TPU v7x, 32 devices: a whole 2x2x4 slice. The times are simulated.
32 devices in a mesh: brick: 16 (over z, y, x), shard: 2 (over core).
Axes of the slice: x: 2, y: 2, z: 4, core: 2. Of those that a mesh axis runs over, the one named last changes fastest.
Arguments:
- velocity: float32 [3, 16, 16384], P(None, 'brick', 'shard'), may hold values from -6 to 6
- particle_mass: float32 [16, 16384], P('brick', 'shard'), may hold values from 0.5 to 2
- particle_volume: float32 [16, 16384], P('brick', 'shard'), may hold values from 0.5 to 2
- lame_first: float32 [16, 16384], P('brick', 'shard'), may hold values from 0.5 to 2
- shear_modulus: float32 [16, 16384], P('brick', 'shard'), may hold values from 0.25 to 1
- stress: float32 [6, 16, 16384], P(None, 'brick', 'shard'), may hold values from -6 to 6
- corner_weights: bfloat16 [16, 128, 64, 128], P('brick', 'shard'), may hold values from 0 to 0.0625
- corner_grads: bfloat16 [3, 16, 128, 64, 128], P(None, 'brick', 'shard'), may hold values from -0.375 to 0.375
- tile_block: int32 [16, 128], P('brick', 'shard'), may hold values from 0 to 255, as said below
- face_blocks: int32 [16, 4, 16], P('brick'), may hold values from 0 to 255, as said below
Outputs:
- new_velocity: float32 [3, 16, 16384], P(None, 'brick', 'shard')
- new_stress: float32 [6, 16, 16384], P(None, 'brick', 'shard')
Inputs may be any that keep to these rules, and one draw needn't show every extreme that they name: Within one brick the 4 x 16 entries are distinct node blocks, and face_blocks[b, k, f] lies among the 16 consecutive node blocks that begin at f * 16. `tile_block`: within one brick the tiles touch min(256, 112) distinct node blocks, among them as many of the face_blocks entries of the brick as that count allows; the other tiles touch blocks of that set again.
All inputs are finite; a program needn't handle non-finite values.
Results may differ from a plain program's by a relative error of at most 0.0011.
Values may be sent and summed in bfloat16 or wider, within the bound.
A program may use at most 64 MiB of HBM per device.

v0:
```python
import jax
import jax.numpy as jnp
import numpy as np
from jax import lax
from jax.sharding import PartitionSpec as P

NB = 256


STEP = 0.5
FLOOR = 1.0


def swapped(value, axis, bit):
    mask = 2**bit
    pairs = [(source, source ^ mask) for source in range(lax.axis_size(axis))]
    return lax.ppermute(value, axis, pairs)


def particle_terms(velocity, particle_mass, particle_volume, stress):
    loads = jnp.concatenate([particle_mass[None], particle_mass[None] * velocity], 0).astype(
        jnp.bfloat16
    )
    pairing = np.array([[0, 3, 5], [3, 1, 4], [5, 4, 2]])
    scaled = (particle_volume[None, None] * stress[pairing]).astype(jnp.bfloat16)
    return (loads, scaled)


def tile_sums(loads, scaled, weights, grads, blocks):
    tile_count, block_nodes, tile_parts = weights.shape
    loads_tiled = loads.reshape(4, tile_count, tile_parts)
    scaled_tiled = scaled.reshape(3, 3, tile_count, tile_parts)
    terms = jnp.einsum("ctp,tnp->tcn", loads_tiled, weights, preferred_element_type=jnp.float32)
    force = jnp.einsum("ijtp,jtnp->tin", scaled_tiled, grads, preferred_element_type=jnp.float32)
    pieces = jnp.concatenate([terms[:, :1], terms[:, 1:] - STEP * force], 1)
    pieces = pieces.reshape(tile_count, 4 * block_nodes)
    return jax.ops.segment_sum(pieces, blocks, num_segments=NB)


def update_nodes(grid, block_ids, rooted):
    rows_here = grid.shape[0]
    block_nodes = grid.shape[1] // 4
    node_mass = grid[:, :block_nodes]
    moment = grid[:, block_nodes:].reshape(rows_here, 3, block_nodes)
    gravity = jnp.array([0.0, 0.0, -1.0], jnp.float32)
    moment = moment + STEP * node_mass[:, None, :] * gravity[None, :, None]
    speeds = moment / jnp.maximum(node_mass, FLOOR)[:, None, :]
    fixed = jnp.logical_and(rooted, block_ids < NB // 8)
    speeds = jnp.where(fixed[:, None, None], jnp.float32(0.0), speeds)
    return speeds.astype(jnp.bfloat16).reshape(rows_here, 3 * block_nodes)


def gather_back(speeds, weights, grads, blocks, stress, lame_first, shear_modulus):
    tile_count, block_nodes, tile_parts = weights.shape
    picked = speeds[blocks].reshape(tile_count, 3, block_nodes)
    moved = jnp.einsum("tcn,tnp->ctp", picked, weights, preferred_element_type=jnp.float32).reshape(
        3, -1
    )
    grad_vel = jnp.einsum(
        "tin,jtnp->ijtp", picked, grads, preferred_element_type=jnp.float32
    ).reshape(3, 3, -1)
    strain = 0.5 * (grad_vel + jnp.transpose(grad_vel, (1, 0, 2)))
    trace_rate = strain[0, 0] + strain[1, 1] + strain[2, 2]
    rate_six = strain[np.array([0, 1, 2, 0, 1, 0]), np.array([0, 1, 2, 1, 2, 2])]
    identity_six = jnp.array([1.0, 1.0, 1.0, 0.0, 0.0, 0.0], jnp.float32)
    updated = stress + STEP * (
        lame_first[None] * trace_rate[None] * identity_six[:, None]
        + 2.0 * shear_modulus[None] * rate_six
    )
    return (moved, updated)


def join_faces(grid, face_blocks):
    faces = face_blocks[0]
    joined = grid
    for cut_index in range(faces.shape[0]):
        chosen = faces[cut_index]
        incoming = swapped(grid[chosen], "brick", cut_index)
        joined = joined.at[chosen].add(incoming)
    return joined


def on_device(
    velocity,
    particle_mass,
    particle_volume,
    lame_first,
    shear_modulus,
    stress,
    corner_weights,
    corner_grads,
    tile_block,
    face_blocks,
):
    loads, scaled = particle_terms(
        velocity[:, 0], particle_mass[0], particle_volume[0], stress[:, 0]
    )
    weights = corner_weights[0]
    grads = corner_grads[:, 0]
    blocks = tile_block[0]
    partial_value = tile_sums(loads, scaled, weights, grads, blocks)
    rooted = lax.axis_index("brick") == 0
    joined = join_faces(partial_value, face_blocks)
    share = lax.psum_scatter(joined, "shard", scatter_dimension=0, tiled=True)
    rows_here = share.shape[0]
    offset = lax.axis_index("shard") * rows_here
    local_speeds = update_nodes(share, offset + jnp.arange(rows_here), rooted)
    speeds = lax.all_gather(local_speeds, "shard", axis=0, tiled=True)
    moved, updated = gather_back(
        speeds, weights, grads, blocks, stress[:, 0], lame_first[0], shear_modulus[0]
    )
    return (moved[:, None], updated[:, None])


def solution(mesh):
    in_specs = (
        P(None, "brick", "shard"),
        P("brick", "shard"),
        P("brick", "shard"),
        P("brick", "shard"),
        P("brick", "shard"),
        P(None, "brick", "shard"),
        P("brick", "shard", None, None),
        P(None, "brick", "shard", None, None),
        P("brick", "shard"),
        P("brick", None, None),
    )
    out_specs = (P(None, "brick", "shard"), P(None, "brick", "shard"))
    return jax.shard_map(
        on_device, mesh=mesh, in_specs=in_specs, out_specs=out_specs, check_vma=False
    )
```

profile of v0, /device:TPU:0, one launch (start us, length us, event | category | flops | bytes accessed | tf_op | source)
XLA Modules:
  0.0 59.8 jit_solution(12282782979239007722)
XLA Ops:
  7.2 0.0 copy-start
  7.2 0.0 copy-start.1
  7.2 0.0 copy-start.2
  7.2 0.0 reduce-scatter.2.cloned.1.call-start
  7.2 1.2 %copy.106 = f32[6,1,8192]{2,0,1:T(8,128)S(1)} copy(f32[6,1,8192]{2,1,0:T(1,128)} %param.23) | data formatting | bytes 393216
  8.4 0.7 %pad_clamp_fusion.5 = s32[1024]{0:T(1024)S(1)} fusion(s32[9]{0:T(128)} %constant.82), kind=kLoop, calls=%fused_computation.60 | loop fusion | flops 1024 | bytes 4132 | tf_op jit(solution)/shard_map/gather | solution.py:25
  9.1 1.4 %gather_fusion = f32[9,8192]{1,0:T(8,128)} fusion(f32[6,8192]{1,0:T(8,128)S(1)} %bitcast.93, s32[1024]{0:T(1024)S(1)} %pad_clamp_fusion.5), kind=kCustom, calls=%fused_computation | custom fusion | bytes 589860 | tf_op jit(solution)/shard_map/gather | solution.py:25
  10.5 1.2 %copy.83 = f32[2,8,64,128]{3,2,1,0:T(8,128)S(1)} copy(f32[2,8,64,128]{3,1,2,0:T(8,128)} %bitcast.94) | data formatting | bytes 1048576
  11.7 0.0 copy-done.1
  11.7 0.0 copy-start.9
  11.8 0.0 copy-done.2
  11.8 0.1 fusion.25
  11.9 1.9 %fusion.17 = f32[64,4,64]{2,1,0:T(4,128)S(1)} fusion(bf16[1,64,64,128]{3,2,1,0:T(8,128)(2,1)} %param.24, bf16[3,64,128]{2,0,1:T(4,128)(2,1)S(1)} %fusion.25, bf16[1,64,128]{2,0,1:T(2,128)(2,1)S(1)} %convert_bitcast_fusion), kind=kOutput, calls=%fused_computation.22 | convolution fusion | flops 4325376 | bytes 1179648 | tf_op jit(solution)/shard_map/ctp,tnp->tcn/dot_general | solution.py:33
  13.8 0.0 copy-done
  13.8 0.0 copy-done.11
  13.8 0.0 copy-start.4
  13.8 1.2 %fusion.13 = f32[64,3,64]{2,1,0:T(4,128)S(1)} fusion(f32[3,3,64,128]{3,2,1,0:T(8,128)S(1)} %bitcast.98, f32[64,128]{1,0:T(8,128)S(1)} %bitcast.103, f32[64,4,64]{2,1,0:T(4,128)S(1)} %fusion.17, bf16[3,1,64,64,128]{4,3,2,1,0:T(8,128)(2,1)S(1)} %copy-done), kind=kOutput, calls=%fused_computation.20 | convolution fusion | flops 9609216 | bytes 3571712 | tf_op jit(solution)/shard_map/ijtp,jtnp->tin/dot_general | solution.py:34
  15.0 0.1 pad_maximum_fusion
  15.1 0.1 reshape.363
  15.3 0.0 copy-start.8
  15.3 0.0 copy-start.5
  15.3 0.0 copy-start.6
  15.3 1.1 %scatter_custom_fusion = f32[256,256]{1,0:T(8,128)S(1)} fusion(s32[64]{0:T(128)} %bitcast.104, f32[64,256]{1,0:T(8,128)S(1)} %reshape.363, f32[]{:T(128)} %constant.23.clone.1), kind=kCustom, calls=%fused_computation.37 | custom fusion | flops 16384 | bytes 262656 | tf_op jit(solution)/shard_map/scatter-add | solution.py:37
  16.4 1.2 %gather_fusion.1 = f32[16,256]{1,0:T(8,128)} fusion(f32[256,256]{1,0:T(8,128)S(1)} %scatter_custom_fusion, s32[1024]{0:T(1024)S(1)} %pad_clamp_fusion.4), kind=kCustom, calls=%fused_computation.1 | custom fusion | bytes 32832 | tf_op jit(solution)/shard_map/gather | solution.py:78
  17.6 3.0 %collective-permute-start = (f32[16,256]{1,0:T(8,128)}, f32[16,256]{1,0:T(8,128)S(1)}, u32[]{:S(2)}, u32[]{:S(2)}) collective-permute-start(f32[16,256]{1,0:T(8,128)} %gather_fusion.1), channel_id=1, source_target_pairs={{0,2},{2,0},{4,6},{6,4},{8,10},{10,8},{12,14},{14,12},{16,18},{18,... | collective-permute-start | bytes 49160 | tf_op jit(solution)/shard_map/ppermute | solution.py:17
  20.6 0.6 gather_fusion.2
  21.2 1.6 %collective-permute-start.1 = (f32[16,256]{1,0:T(8,128)S(1)}, f32[16,256]{1,0:T(8,128)S(1)}, u32[]{:S(2)}, u32[]{:S(2)}) collective-permute-start(f32[16,256]{1,0:T(8,128)S(1)} %gather_fusion.2), channel_id=1, source_target_pairs={{0,4},{2,6},{4,0},{6,2},{8,12},{10,14},{12,8},{14,10},{16,20},{18,... | collective-permute-start | bytes 49160 | tf_op jit(solution)/shard_map/ppermute | solution.py:17
  22.8 0.0 copy-done.8
  22.8 0.6 gather_fusion.3
  23.3 1.6 %collective-permute-start.2 = (f32[16,256]{1,0:T(8,128)S(1)}, f32[16,256]{1,0:T(8,128)S(1)}, u32[]{:S(2)}, u32[]{:S(2)}) collective-permute-start(f32[16,256]{1,0:T(8,128)S(1)} %gather_fusion.3), channel_id=1, source_target_pairs={{0,8},{2,10},{4,12},{6,14},{8,0},{10,2},{12,4},{14,6},{16,24},{18,... | collective-permute-start | bytes 49160 | tf_op jit(solution)/shard_map/ppermute | solution.py:17
  25.0 0.6 gather_fusion.4
  25.6 2.7 %collective-permute-start.3 = (f32[16,256]{1,0:T(8,128)S(1)}, f32[16,256]{1,0:T(8,128)S(1)}, u32[]{:S(2)}, u32[]{:S(2)}) collective-permute-start(f32[16,256]{1,0:T(8,128)S(1)} %gather_fusion.4), channel_id=1, source_target_pairs={{0,16},{2,18},{4,20},{6,22},{8,24},{10,26},{12,28},{14,30},{16,0},... | collective-permute-start | bytes 49160 | tf_op jit(solution)/shard_map/ppermute | solution.py:17
  28.2 0.0 collective-permute-done
  28.2 0.9 %scatter_fusion = f32[256,256]{1,0:T(8,128)S(1)} fusion(f32[256,256]{1,0:T(8,128)S(1)} %scatter_custom_fusion, s32[16]{0:T(128)} %copy-done.8, f32[16,256]{1,0:T(8,128)S(1)} %collective-permute-done), kind=kCustom, calls=%fused_computation.8 | custom fusion | flops 4096 | bytes 49216 | tf_op jit(solution)/shard_map/scatter-add | solution.py:79
  29.2 0.0 collective-permute-done.1
  29.2 0.9 %scatter_fusion.1 = f32[256,256]{1,0:T(8,128)S(1)} fusion(f32[256,256]{1,0:T(8,128)S(1)} %scatter_fusion, s32[16]{0:T(128)} %copy-done.7, f32[16,256]{1,0:T(8,128)S(1)} %collective-permute-done.1), kind=kCustom, calls=%fused_computation.9 | custom fusion | flops 4096 | bytes 49216 | tf_op jit(solution)/shard_map/scatter-add | solution.py:79
  30.1 0.0 collective-permute-done.2
  30.1 0.9 %scatter_fusion.2 = f32[256,256]{1,0:T(8,128)S(1)} fusion(f32[256,256]{1,0:T(8,128)S(1)} %scatter_fusion.1, s32[16]{0:T(128)} %copy-done.6, f32[16,256]{1,0:T(8,128)S(1)} %collective-permute-done.2), kind=kCustom, calls=%fused_computation.10 | custom fusion | flops 4096 | bytes 49216 | tf_op jit(solution)/shard_map/scatter-add | solution.py:79
  31.1 0.0 collective-permute-done.3
  31.1 0.9 %scatter_fusion.3 = f32[256,256]{1,0:T(8,128)S(1)} fusion(f32[256,256]{1,0:T(8,128)S(1)} %scatter_fusion.2, s32[16]{0:T(128)} %copy-done.5, f32[16,256]{1,0:T(8,128)S(1)} %collective-permute-done.3), kind=kCustom, calls=%fused_computation.11 | custom fusion | flops 4096 | bytes 49216 | tf_op jit(solution)/shard_map/scatter-add | solution.py:79
  32.0 0.8 %copy.67 = f32[256,256]{0,1:T(8,128)} copy(f32[256,256]{1,0:T(8,128)S(1)} %scatter_fusion.3) | data formatting | bytes 524288 | tf_op jit(solution)/shard_map/scatter-add | solution.py:79
  32.8 0.0 reduce-scatter.2.cloned.1.call-update
  32.9 0.6 %broadcast_multiply_fusion = f32[1,8192]{1,0:T(1,128)} fusion(f32[1,8192]{1,0:T(1,128)S(1)} %copy-done.4), kind=kLoop, calls=%fused_computation.54 | loop fusion | flops 8192 | bytes 65536 | tf_op jit(solution)/shard_map/mul | solution.py:68
  33.5 0.7 %mul.138 = f32[3,64]{1,0:T(4,128)S(1)} broadcast(f32[3]{0:T(128)} %constant.15.clone), dimensions={0} | broadcast | bytes 780 | tf_op jit(solution)/shard_map/mul | solution.py:46
  34.3 0.1 mul.139
  34.3 0.7 %fusion.40 = s32[64]{0:T(128)S(1)} fusion(s32[1,64]{1,0:T(1,128)} %param.26), kind=kLoop, calls=%fused_computation.71 | loop fusion | flops 192 | bytes 512 | tf_op jit(solution)/shard_map/select_n | solution.py:55
  35.0 3.3 %reduce-scatter.2.cloned.1.call-done = f32[128,256]{0,1:T(8,128)} async-done(((f32[256,256]{0,1:T(8,128)}), f32[128,256]{0,1:T(8,128)}) %reduce-scatter.2.cloned.1.call-update) | async-done | bytes 131088 | tf_op jit(solution)/shard_map/reduce_scatter | solution.py:104
  38.3 0.8 %slice_multiply_fusion = (f32[128,64]{0,1:T(8,128)S(1)}, f32[128,64]{0,1:T(8,128)S(1)}) fusion(f32[128,256]{0,1:T(8,128)} %reduce-scatter.2.cloned.1.call-done), kind=kLoop, calls=%fused_computation.53 | loop fusion | flops 16384 | bytes 98304 | tf_op jit(solution)/shard_map/mul | solution.py:46
  39.1 1.0 %fusion.30 = bf16[128,192]{0,1:T(8,128)(2,1)S(1)} fusion(f32[128,256]{0,1:T(8,128)} %reduce-scatter.2.cloned.1.call-done, f32[128,64]{0,1:T(8,128)S(1)} %get-tuple-element.11, f32[192]{0:T(256)S(1)} %mul.139, f32[128,64]{0,1:T(8,128)S(1)} %get-tuple-element.10, pred[128]{0:T(512)(128)(4,1)S(1)} %compare_and_fusion), kind=kLoop, calls=%fused_computation.43 | loop fusion | flops 122880 | bytes 213888 | tf_op jit(solution)/shard_map/convert_element_type | solution.py:50
  40.1 1.9 %all_gather.3 = bf16[256,192]{0,1:T(8,128)(2,1)S(1)} all-gather(bf16[128,192]{0,1:T(8,128)(2,1)S(1)} %fusion.30), channel_id=1, replica_groups=mesh['brick'=16,'shard'=2] {'shard'}, dimensions={0}, use_global_device_ids=true | all-gather | bytes 147456 | tf_op jit(solution)/shard_map/all_gather | solution.py:108
  42.0 0.1 copy.68
  42.1 0.7 %gather_fusion.5 = bf16[64,192]{1,0:T(8,128)(2,1)S(1)} fusion(bf16[256,192]{1,0:T(8,128)(2,1)S(1)} %copy.68, s32[1024]{0:T(1024)S(1)} %pad_clamp_fusion), kind=kCustom, calls=%fused_computation.5 | custom fusion | bytes 49408 | tf_op jit(solution)/shard_map/gather | solution.py:55
  42.8 0.1 copy.69
  42.9 0.1 copy.70
  43.0 1.6 %convolution_bitcast_fusion = f32[3,1,8192]{2,0,1:T(4,128)S(1)} fusion(bf16[64,3,64]{2,1,0:T(4,128)(2,1)S(1)} %copy.70, bf16[1,64,64,128]{3,2,1,0:T(8,128)(2,1)} %param.24), kind=kOutput, calls=%fused_computation.12 | convolution fusion | flops 3145728 | bytes 1171456 | tf_op jit(solution)/shard_map/tcn,tnp->ctp/dot_general | solution.py:56
  44.6 0.8 %copy.76 = f32[3,1,8192]{2,1,0:T(1,128)} copy(f32[3,1,8192]{2,0,1:T(4,128)S(1)} %convolution_bitcast_fusion) | data formatting | bytes 196608
  45.4 0.1 copy.79
  45.5 0.7 %fusion.4 = f32[3,3,64,128]{3,0,1,2:T(4,128)S(1)} fusion(bf16[64,3,64,1]{2,1,3,0:T(4,128)(2,1)S(1)} %copy.79, bf16[3,1,64,64,128]{4,3,2,1,0:T(8,128)(2,1)S(1)} %copy-done), kind=kOutput, calls=%fused_computation.17 | convolution fusion | flops 9437184 | bytes 3465216 | tf_op jit(solution)/shard_map/tin,jtnp->ijtp/dot_general | solution.py:59
  46.2 0.9 %reshape.304 = f32[3,3,8192]{2,1,0:T(4,128)} reshape(f32[3,3,64,128]{3,2,1,0:T(8,128)S(1)} %copy.73) | data formatting | bytes 589824 | tf_op jit(solution)/shard_map/reshape | solution.py:61
  47.1 1.4 %fusion.19 = f32[3,3,8192]{2,1,0:T(4,128)S(1)} fusion(f32[3,3,8192]{2,1,0:T(4,128)} %reshape.304), kind=kLoop, calls=%fused_computation.25 | loop fusion | flops 147456 | bytes 589824 | tf_op jit(solution)/shard_map/mul | solution.py:62
  48.4 1.6 %gather_fusion.6 = f32[6,8192]{1,0:T(8,128)} fusion(f32[3,3,8192]{2,1,0:T(4,128)S(1)} %fusion.19, s32[6]{0:T(128)S(1)} %copy-done.3), kind=kCustom, calls=%fused_computation.6 | custom fusion | bytes 393264 | tf_op jit(solution)/shard_map/gather | solution.py:64
  50.1 0.8 %fusion.35 = f32[1,8192]{1,0:T(1,128)S(1)} fusion(f32[1,8192]{1,0:T(1,128)} %param.21, f32[3,3,8192]{2,1,0:T(4,128)S(1)} %fusion.19), kind=kLoop, calls=%fused_computation.49 | loop fusion | flops 24576 | bytes 163840 | tf_op jit(solution)/shard_map/mul | solution.py:67
  50.9 1.2 %copy_add_fusion = f32[6,1,8192]{2,0,1:T(8,128)S(1)} fusion(f32[6,1,8192]{2,1,0:T(1,128)} %param.23, f32[6,8192]{1,0:T(8,128)} %gather_fusion.6, f32[8192]{0:T(1024)} %bitcast.101, f32[6]{0:T(128)S(1)} %copy-done.10, f32[8192]{0:T(1024)S(1)} %bitcast.100), kind=kLoop, calls=%fused_computation.28 | loop fusion | flops 245760 | bytes 655384 | tf_op jit(solution)/shard_map/add | solution.py:66
  52.1 0.9 %copy.77 = f32[6,1,8192]{2,1,0:T(1,128)} copy(f32[6,1,8192]{2,0,1:T(8,128)S(1)} %copy_add_fusion) | data formatting | bytes 393216
  (22 shorter events, 0.2 us)
Async XLA Ops:
  7.2 6.6 %copy-start = (bf16[3,1,64,64,128]{4,3,2,1,0:T(8,128)(2,1)S(1)}, bf16[3,1,64,64,128]{4,3,2,1,0:T(8,128)(2,1)}, u32[]{:S(2)}) copy-start(bf16[3,1,64,64,128]{4,3,2,1,0:T(8,128)(2,1)} %param.25) | copy-start | bytes 9437188
  7.2 4.5 %copy-start.1 = (f32[1,8192]{1,0:T(1,128)S(1)}, f32[1,8192]{1,0:T(1,128)}, u32[]{:S(2)}) copy-start(f32[1,8192]{1,0:T(1,128)} %param.19) | copy-start | bytes 98308
  7.2 4.6 %copy-start.2 = (f32[3,1,8192]{2,1,0:T(1,128)S(1)}, f32[3,1,8192]{2,1,0:T(1,128)}, u32[]{:S(2)}) copy-start(f32[3,1,8192]{2,1,0:T(1,128)} %param.18) | copy-start | bytes 294916
  7.2 31.1 %reduce-scatter.2.cloned.1.call-start = ((), (), s32[]{:S(2)}) async-start(), calls=%async_computation.1 | async-start | bytes 393216 | tf_op jit(solution)/shard_map/reduce_scatter | solution.py:104
  10.5 3.3 %copy-start.11 = (f32[1,8192]{1,0:T(1,128)S(1)}, f32[1,8192]{1,0:T(1,128)}, u32[]{:S(2)}) copy-start(f32[1,8192]{1,0:T(1,128)} %param.20) | copy-start | bytes 98308
  11.7 3.5 %copy-start.9 = (s32[1,4,16]{2,1,0:T(4,128)S(1)}, s32[1,4,16]{2,1,0:T(4,128)}, u32[]{:S(2)}) copy-start(s32[1,4,16]{2,1,0:T(4,128)} %param.27) | copy-start | bytes 772
  13.8 19.1 %copy-start.4 = (f32[1,8192]{1,0:T(1,128)S(1)}, f32[1,8192]{1,0:T(1,128)}, u32[]{:S(2)}) copy-start(f32[1,8192]{1,0:T(1,128)} %param.22) | copy-start | bytes 98308
  15.3 7.5 %copy-start.7 = (s32[16]{0:T(128)}, s32[16]{0:T(128)S(1)}, u32[]{:S(2)}) copy-start(s32[16]{0:T(128)S(1)} %get-tuple-element.13) | copy-start | bytes 196
  15.3 7.5 %copy-start.8 = (s32[16]{0:T(128)}, s32[16]{0:T(128)S(1)}, u32[]{:S(2)}) copy-start(s32[16]{0:T(128)S(1)} %get-tuple-element.14) | copy-start | bytes 196
  15.3 9.7 %copy-start.5 = (s32[16]{0:T(128)}, s32[16]{0:T(128)S(1)}, u32[]{:S(2)}) copy-start(s32[16]{0:T(128)S(1)} %get-tuple-element.12) | copy-start | bytes 196
  15.3 9.7 %copy-start.6 = (s32[16]{0:T(128)}, s32[16]{0:T(128)S(1)}, u32[]{:S(2)}) copy-start(s32[16]{0:T(128)S(1)} %get-tuple-element.15) | copy-start | bytes 196
  17.6 10.6 %collective-permute-start = (f32[16,256]{1,0:T(8,128)}, f32[16,256]{1,0:T(8,128)S(1)}, u32[]{:S(2)}, u32[]{:S(2)}) collective-permute-start(f32[16,256]{1,0:T(8,128)} %gather_fusion.1), channel_id=1, source_target_pairs={{0,2},{2,0},{4,6},{6,4},{8,10},{10,8},{12,14},{14,12},{16,18},{18,... | collective-permute-start | bytes 49160 | tf_op jit(solution)/shard_map/ppermute | solution.py:17
  21.2 8.0 %collective-permute-start.1 = (f32[16,256]{1,0:T(8,128)S(1)}, f32[16,256]{1,0:T(8,128)S(1)}, u32[]{:S(2)}, u32[]{:S(2)}) collective-permute-start(f32[16,256]{1,0:T(8,128)S(1)} %gather_fusion.2), channel_id=1, source_target_pairs={{0,4},{2,6},{4,0},{6,2},{8,12},{10,14},{12,8},{14,10},{16,20},{18,... | collective-permute-start | bytes 49160 | tf_op jit(solution)/shard_map/ppermute | solution.py:17
  23.3 6.8 %collective-permute-start.2 = (f32[16,256]{1,0:T(8,128)S(1)}, f32[16,256]{1,0:T(8,128)S(1)}, u32[]{:S(2)}, u32[]{:S(2)}) collective-permute-start(f32[16,256]{1,0:T(8,128)S(1)} %gather_fusion.3), channel_id=1, source_target_pairs={{0,8},{2,10},{4,12},{6,14},{8,0},{10,2},{12,4},{14,6},{16,24},{18,... | collective-permute-start | bytes 49160 | tf_op jit(solution)/shard_map/ppermute | solution.py:17
  25.6 5.5 %collective-permute-start.3 = (f32[16,256]{1,0:T(8,128)S(1)}, f32[16,256]{1,0:T(8,128)S(1)}, u32[]{:S(2)}, u32[]{:S(2)}) collective-permute-start(f32[16,256]{1,0:T(8,128)S(1)} %gather_fusion.4), channel_id=1, source_target_pairs={{0,16},{2,18},{4,20},{6,22},{8,24},{10,26},{12,28},{14,30},{16,0},... | collective-permute-start | bytes 49160 | tf_op jit(solution)/shard_map/ppermute | solution.py:17
  44.6 3.8 %copy-start.3 = (s32[6]{0:T(128)S(1)}, s32[6]{0:T(128)}, u32[]{:S(2)}) copy-start(s32[6]{0:T(128)} %constant.90) | copy-start | bytes 76
  46.1 4.8 %copy-start.10 = (f32[6]{0:T(128)S(1)}, f32[6]{0:T(128)}, u32[]{:S(2)}) copy-start(f32[6]{0:T(128)} %constant.54.clone) | copy-start | bytes 76
Sparse Core Ops, SparseCore 0:
  33.0 5.2 reduce-scatter.1
where the time goes:
time: 60.3 us; the launch traced here: 59.8 us
  between operations  14.3 us (24%)
  local copies, waits for them, and re-layouts  13.9 us (23%)
  other arithmetic  12.2 us (20%)
  starting transfers between devices  8.89 us (15%)
  matrix products  5.32 us (9%)
  waiting for transfers between devices  3.32 us (6%)
  blocking collectives  1.91 us (3%)
    ppermute x4, starting transfers between devices, swapped(): return lax.ppermute(value, axis, pairs)  8.85 us
    unnamed x29, local copies, waits for them, and re-layouts  4.07 us
    scatter-add x4, other arithmetic, join_faces(): joined = joined.at[chosen].add(incoming)  3.72 us
    reduce_scatter x1, waiting for transfers between devices, on_device(): share = lax.psum_scatter(joined, 'shard', scatter_dimension=0, tiled=True)  3.29 us
    gather x4, local copies, waits for them, and re-layouts, join_faces(): incoming = swapped(grid[chosen], 'brick', cut_index)  2.9 us
    all_gather x1, blocking collectives, on_device(): speeds = lax.all_gather(local_speeds, 'shard', axis=0, tiled=True)  1.91 us
    dot_general x1, matrix products, tile_sums(): jnp.einsum('ctp,tnp->tcn', loads_tiled, weights, preferred_element_type=j...  1.86 us
    gather x1, local copies, waits for them, and re-layouts, gather_back(): strain[np.array([0, 1, 2, 0, 1, 0]), np.array([0, 1, 2, 1, 2, 2])]  1.62 us
  transfers between devices with their start and end apart: 5, of which 1 were waited for; matrix products, arithmetic and copies ran while one was open for 11% of the time, Pallas kernels for 0%

commit v1 on v0

v1 whole, which is shorter than its diff:
```python
import functools

import jax
import jax.numpy as jnp
from jax import lax
from jax.experimental import pallas as pl
from jax.experimental.pallas import tpu as pltpu
from jax.sharding import PartitionSpec as P

NB = 256
STEP = 0.5
FLOOR = 1.0
MESH = pl.DeviceIdType.MESH
GROUP = 8
PAIRING = ((0, 3, 5), (3, 1, 4), (5, 4, 2))
SIX = ((0, 0), (1, 1), (2, 2), (0, 1), (1, 2), (0, 2))


def thirds(value):
    high = value.astype(jnp.bfloat16)
    rest = value - high.astype(jnp.float32)
    middle = rest.astype(jnp.bfloat16)
    low = (rest - middle.astype(jnp.float32)).astype(jnp.bfloat16)
    return jnp.concatenate([high, middle, low], 1)


def select_sum(chosen, value):
    wide = value.shape[1]
    out = jnp.dot(chosen, thirds(value), preferred_element_type=jnp.float32)
    return out[:, :wide] + out[:, wide : 2 * wide] + out[:, 2 * wide :]


def column_of(row):
    size = row.shape[1]
    square = jnp.broadcast_to(row, (size, size))
    rows = lax.broadcasted_iota(jnp.int32, (size, size), 0)
    columns = lax.broadcasted_iota(jnp.int32, (size, size), 1)
    return jnp.sum(jnp.where(rows == columns, square, 0.0), axis=1, keepdims=True)


def row_of(column):
    size = column.shape[0]
    square = jnp.broadcast_to(column, (size, size))
    rows = lax.broadcasted_iota(jnp.int32, (size, size), 0)
    columns = lax.broadcasted_iota(jnp.int32, (size, size), 1)
    return jnp.sum(jnp.where(rows == columns, square, 0.0), axis=0, keepdims=True)


def equal(column, row):
    return jnp.where(column == row, 1.0, 0.0).astype(jnp.bfloat16)


def kernel(
    velocity,
    mass,
    volume,
    lame,
    shear,
    stress,
    weights_in,
    grads_in,
    blocks,
    faces,
    moved_out,
    stress_out,
    weights,
    grads,
    own_sums,
    face_sums,
    other_sums,
    other_blocks,
    face_in,
    load_sem,
    sum_sems,
    block_sems,
    face_send,
    face_recv,
):
    brick = lax.axis_index("brick")
    shard = lax.axis_index("shard")
    tiles, nodes, parts = weights.shape
    cuts, face_count = faces.shape
    groups = tiles // GROUP

    loads = []
    for g in range(groups):
        rows = pl.ds(g * GROUP, GROUP)
        pair = (
            pltpu.make_async_copy(weights_in.at[rows], weights.at[rows], load_sem.at[g, 0]),
            pltpu.make_async_copy(grads_in.at[:, rows], grads.at[:, rows], load_sem.at[g, 1]),
        )
        for copy in pair:
            copy.start()
        loads.append(pair)

    sibling = (brick, 1 - shard)
    partners = []
    for k in range(cuts):
        bit = 2**k
        partner = brick + (1 - 2 * ((brick // bit) % 2)) * bit
        partners.append(((partner, shard), (partner, 1 - shard)))
    barrier = pltpu.get_barrier_semaphore()
    greeted = [sibling] + [device for both in partners for device in both]
    for device in greeted:
        pl.semaphore_signal(barrier, inc=1, device_id=device, device_id_type=MESH)

    lanes = lax.broadcasted_iota(jnp.int32, (GROUP, GROUP * nodes), 1)
    sublanes = lax.broadcasted_iota(jnp.int32, (GROUP, GROUP * nodes), 0)
    own_node = lanes // nodes == sublanes
    width = 2 * nodes

    block_row = blocks[...].astype(jnp.float32)
    block_column = column_of(block_row)
    face_rows = faces[...].astype(jnp.float32)
    face_column = jnp.concatenate([column_of(face_rows[k : k + 1]) for k in range(cuts)], 0)
    face_row = row_of(face_column)
    face_of_tile = equal(block_column, face_row)
    tile_of_face = equal(face_column, block_row)
    same_here = equal(block_column, block_row)

    first_half = lax.broadcasted_iota(jnp.int32, (GROUP, width), 1) < nodes
    for g in range(groups):
        rows = pl.ds(g * GROUP, GROUP)
        for copy in loads[g]:
            copy.wait()
        m = mass[rows]
        zero = jnp.zeros_like(m)
        columns = [jnp.concatenate([m] + [m * velocity[c, rows] for c in range(3)], 0)]
        vol = volume[rows]
        scaled = [(-STEP) * (vol * stress[s, rows]) for s in range(6)]
        for j in range(3):
            columns.append(jnp.concatenate([zero] + [scaled[PAIRING[i][j]] for i in range(3)], 0))
        left = jnp.concatenate([column.astype(jnp.bfloat16) for column in columns], 1)
        right = jnp.concatenate(
            [weights[rows].reshape(GROUP * nodes, parts)]
            + [grads[j, rows].reshape(GROUP * nodes, parts) for j in range(3)],
            1,
        )
        out = lax.dot_general(
            left, right, (((1,), (1,)), ((), ())), preferred_element_type=jnp.float32
        )
        twice = []
        for c in range(4):
            piece = jnp.where(own_node, out[c * GROUP : (c + 1) * GROUP], 0.0)
            total = piece[:, :width]
            for q in range(1, GROUP // 2):
                total = total + piece[:, q * width : (q + 1) * width]
            twice.append(total + pltpu.roll(total, nodes, 1))
        own_sums[rows, :width] = jnp.where(first_half, twice[0], twice[1])
        own_sums[rows, width:] = jnp.where(first_half, twice[2], twice[3])

    pieces = own_sums[...]
    face_sums[...] = select_sum(tile_of_face, pieces)

    pl.semaphore_wait(barrier, len(greeted))
    copies = [
        pltpu.make_async_remote_copy(
            src_ref=own_sums,
            dst_ref=other_sums,
            send_sem=sum_sems.at[0],
            recv_sem=sum_sems.at[1],
            device_id=sibling,
            device_id_type=MESH,
        ),
        pltpu.make_async_remote_copy(
            src_ref=blocks,
            dst_ref=other_blocks,
            send_sem=block_sems.at[0],
            recv_sem=block_sems.at[1],
            device_id=sibling,
            device_id_type=MESH,
        ),
    ]
    for k in reversed(range(cuts)):
        for r in range(2):
            rows = pl.ds(k * face_count, face_count)
            copies.append(
                pltpu.make_async_remote_copy(
                    src_ref=face_sums.at[rows],
                    dst_ref=face_in.at[r, rows],
                    send_sem=face_send.at[r, k],
                    recv_sem=face_recv.at[r, k],
                    device_id=partners[k][r],
                    device_id_type=MESH,
                )
            )
    for copy in copies:
        copy.start()
    total = select_sum(same_here, pieces)
    copies[0].wait()
    copies[1].wait()
    same_there = equal(block_column, other_blocks[...].astype(jnp.float32))
    total = total + select_sum(same_there, other_sums[...])
    for copy in copies[2:]:
        copy.wait()
    total = total + select_sum(face_of_tile, face_in[0] + face_in[1])

    half = lax.broadcasted_iota(jnp.int32, (tiles, width), 1) < nodes
    one, two = total[:, :width], total[:, width:]
    one_turned, two_turned = pltpu.roll(one, nodes, 1), pltpu.roll(two, nodes, 1)
    node_mass = jnp.where(half, one, one_turned)
    moment = [
        jnp.where(half, one_turned, one),
        jnp.where(half, two, two_turned),
        jnp.where(half, two_turned, two) - STEP * node_mass,
    ]
    floor = jnp.maximum(node_mass, FLOOR)
    bound = jnp.where(brick == 0, float(NB // 8), 0.0)
    fixed = block_column < bound
    speeds = [jnp.where(fixed, 0.0, q / floor) for q in moment]

    for g in range(groups):
        rows = pl.ds(g * GROUP, GROUP)
        left = jnp.concatenate(
            [
                jnp.where(
                    own_node,
                    jnp.concatenate([s[g * GROUP : (g + 1) * GROUP]] * (GROUP // 2), 1),
                    0.0,
                )
                for s in speeds
            ],
            0,
        ).astype(jnp.bfloat16)
        right = jnp.concatenate(
            [weights[rows].reshape(GROUP * nodes, parts)]
            + [grads[j, rows].reshape(GROUP * nodes, parts) for j in range(3)],
            1,
        )
        out = jnp.dot(left, right, preferred_element_type=jnp.float32)

        def block(i, q):
            return out[i * GROUP : (i + 1) * GROUP, q * parts : (q + 1) * parts]

        for c in range(3):
            moved_out[c, rows] = block(c, 0)
        trace = block(0, 1) + block(1, 2) + block(2, 3)
        bulk = STEP * (lame[rows] * trace)
        twist = (2.0 * STEP) * shear[rows]
        for s, (i, j) in enumerate(SIX):
            if i == j:
                stress_out[s, rows] = stress[s, rows] + (bulk + twist * block(i, j + 1))
            else:
                rate = 0.5 * (block(i, j + 1) + block(j, i + 1))
                stress_out[s, rows] = stress[s, rows] + twist * rate


def on_device(
    velocity,
    particle_mass,
    particle_volume,
    lame_first,
    shear_modulus,
    stress,
    corner_weights,
    corner_grads,
    tile_block,
    face_blocks,
):
    weights, grads = corner_weights[0], corner_grads[:, 0]
    tiles, nodes, parts = weights.shape
    cuts, face_count = face_blocks.shape[1:]
    faces = cuts * face_count
    groups = tiles // GROUP
    vmem = pl.BlockSpec(memory_space=pltpu.VMEM)
    hbm = pl.BlockSpec(memory_space=pl.ANY)
    f32 = jnp.float32
    dma = pltpu.SemaphoreType.DMA
    moved, updated = pl.pallas_call(
        kernel,
        out_shape=(
            jax.ShapeDtypeStruct((3, tiles, parts), f32),
            jax.ShapeDtypeStruct((6, tiles, parts), f32),
        ),
        in_specs=[vmem] * 6 + [hbm] * 2 + [vmem] * 2,
        out_specs=(vmem, vmem),
        scratch_shapes=[
            pltpu.VMEM((tiles, nodes, parts), jnp.bfloat16),
            pltpu.VMEM((3, tiles, nodes, parts), jnp.bfloat16),
            pltpu.VMEM((tiles, 4 * nodes), f32),
            pltpu.VMEM((faces, 4 * nodes), f32),
            pltpu.VMEM((tiles, 4 * nodes), f32),
            pltpu.VMEM((1, tiles), jnp.int32),
            pltpu.VMEM((2, faces, 4 * nodes), f32),
            dma((groups, 2)),
            dma((2,)),
            dma((2,)),
            dma((2, cuts)),
            dma((2, cuts)),
        ],
        compiler_params=pltpu.CompilerParams(collective_id=0, has_side_effects=True),
        name="step",
    )(
        velocity.reshape(3, tiles, parts),
        particle_mass.reshape(tiles, parts),
        particle_volume.reshape(tiles, parts),
        lame_first.reshape(tiles, parts),
        shear_modulus.reshape(tiles, parts),
        stress.reshape(6, tiles, parts),
        weights,
        grads,
        tile_block,
        face_blocks[0],
    )
    return moved.reshape(3, 1, -1), updated.reshape(6, 1, -1)


def solution(mesh):
    in_specs = (
        P(None, "brick", "shard"),
        P("brick", "shard"),
        P("brick", "shard"),
        P("brick", "shard"),
        P("brick", "shard"),
        P(None, "brick", "shard"),
        P("brick", "shard", None, None),
        P(None, "brick", "shard", None, None),
        P("brick", "shard"),
        P("brick", None, None),
    )
    out_specs = (P(None, "brick", "shard"), P(None, "brick", "shard"))
    return jax.shard_map(
        on_device, mesh=mesh, in_specs=in_specs, out_specs=out_specs, check_vma=False
    )
```

time: 60.3 us -> 16.9 us (0.28)
  between operations: 14.3 us -> 0.64 us
  Pallas kernels: 0 us -> 12.9 us
  other arithmetic: 12.2 us -> 0 us
  local copies, waits for them, and re-layouts: 13.9 us -> 3.16 us
  starting transfers between devices: 8.89 us -> 0 us
  matrix products: 5.32 us -> 0 us
  waiting for transfers between devices: 3.32 us -> 0 us
  blocking collectives: 1.91 us -> 0 us
    pallas_call x0 -> x1, Pallas kernels: none -> 12.9 us  [on_device(): pl.pallas_call(kernel, out_shape=(jax.ShapeDtypeStruct((3, tiles, parts),...]
    ppermute x4 -> x0, starting transfers between devices: 8.85 us -> none  [swapped(): return lax.ppermute(value, axis, pairs)]
    gather x8 -> x0, local copies, waits for them, and re-layouts: 6.74 us -> none  [the longest x4 2.9 us: join_faces(): incoming = swapped(grid[chosen], 'brick', cut_index)]
    dot_general x4 -> x0, matrix products: 5.32 us -> none  [the longest x1 1.86 us: tile_sums(): jnp.einsum('ctp,tnp->tcn', loads_tiled, weights, preferred_element_type=j...]
    scatter-add x5 -> x0, other arithmetic: 4.83 us -> none  [the longest x4 3.72 us: join_faces(): joined = joined.at[chosen].add(incoming)]
    mul x4 -> x0, other arithmetic: 3.62 us -> none  [the longest x1 1.36 us: gather_back(): strain = 0.5 * (grad_vel + jnp.transpose(grad_vel, (1, 0, 2)))]
    reduce_scatter x1 -> x0, waiting for transfers between devices: 3.29 us -> none  [on_device(): share = lax.psum_scatter(joined, 'shard', scatter_dimension=0, tiled=True)]
    all_gather x1 -> x0, blocking collectives: 1.91 us -> none  [on_device(): speeds = lax.all_gather(local_speeds, 'shard', axis=0, tiled=True)]
  transfers between devices with their start and end apart: 5 -> 0, of which waited for: 1 -> 0; matrix products, arithmetic and copies ran while one was open for 11% -> 0% of each run, Pallas kernels for 0% -> 0%
where the time goes in v1:
time: 16.9 us; the launch traced here: 16.7 us
  Pallas kernels  12.9 us (76%)
  local copies, waits for them, and re-layouts  3.16 us (19%)
  between operations  0.64 us (4%)
    pallas_call x1, Pallas kernels, on_device(): pl.pallas_call(kernel, out_shape=(jax.ShapeDtypeStruct((3, tiles, parts),...  12.9 us
    unnamed x2, local copies, waits for them, and re-layouts  3.16 us

profile of v1, /device:TPU:0, one launch (start us, length us, event | category | flops | bytes accessed | tf_op | source)
XLA Modules:
  0.0 16.7 jit_solution(17917545709911570390)
XLA Ops:
  0.6 12.9 %step.1 = (f32[3,64,128]{2,1,0:T(8,128)}, f32[6,64,128]{2,1,0:T(8,128)}) custom-call(f32[3,64,128]{2,1,0:T(8,128)} %bitcast.16, f32[64,128]{1,0:T(8,128)} %bitcast.17, f32[64,128]{1,0:T(8,128)} %bitcast.18, f32[64,128]{1,0:T(8,128)} %bitcast.19, f32[64,128]{1,0:T(8,128)} %bitcast.20, f32[6,64,128]{2,1,0:T(8,128)} %bitcast.13, bf16[64,64,128]{2,1,0:T(8,128)(2,1)} %bitcast.12, ...), custom_call_target="tpu_custom_call" | custom-call | tf_op jit(solution)/shard_map/step/pallas_call | solution.py:269
  13.5 1.5 %copy.18 = f32[3,1,8192]{2,1,0:T(1,128)} copy(f32[3,1,8192]{2,1,0:T(1,128)} %bitcast.15) | data formatting | bytes 196608
  15.1 1.6 %copy.19 = f32[6,1,8192]{2,1,0:T(1,128)} copy(f32[6,1,8192]{2,1,0:T(1,128)} %bitcast.14) | data formatting | bytes 393216

commit v2 on v1

--- a/solution.py
+++ b/solution.py
@@ -1,5 +1,3 @@
-import functools
-
 import jax
 import jax.numpy as jnp
 from jax import lax
@@ -12,6 +10,8 @@
 FLOOR = 1.0
 MESH = pl.DeviceIdType.MESH
 GROUP = 8
+SPANS = 4
+VMEM_LIMIT = 16 * 2**20
 PAIRING = ((0, 3, 5), (3, 1, 4), (5, 4, 2))
 SIX = ((0, 0), (1, 1), (2, 2), (0, 1), (1, 2), (0, 2))
 
@@ -50,26 +50,34 @@
     return jnp.where(column == row, 1.0, 0.0).astype(jnp.bfloat16)
 
 
-def kernel(
+def exchange_kernel(
+    velocity_in,
+    mass_in,
+    volume_in,
+    lame_in,
+    shear_in,
+    stress_in,
+    weights_in,
+    grads_in,
+    blocks_in,
+    faces_in,
+    speeds_out,
+    weights,
+    grads,
+    stress,
+    lame,
+    shear,
     velocity,
     mass,
     volume,
-    lame,
-    shear,
-    stress,
-    weights_in,
-    grads_in,
     blocks,
     faces,
-    moved_out,
-    stress_out,
-    weights,
-    grads,
     own_sums,
     face_sums,
     other_sums,
     other_blocks,
     face_in,
+    small_sem,
     load_sem,
     sum_sems,
     block_sems,
@@ -82,6 +90,17 @@
     cuts, face_count = faces.shape
     groups = tiles // GROUP
 
+    small = []
+    for source, target in (
+        (mass_in, mass),
+        (velocity_in, velocity),
+        (volume_in, volume),
+        (stress_in, stress),
+        (blocks_in, blocks),
+        (faces_in, faces),
+    ):
+        small.append(pltpu.make_async_copy(source, target, small_sem.at[len(small)]))
+        small[-1].start()
     loads = []
     for g in range(groups):
         rows = pl.ds(g * GROUP, GROUP)
@@ -92,6 +111,12 @@
         for copy in pair:
             copy.start()
         loads.append(pair)
+    late = []
+    for source, target in ((lame_in, lame), (shear_in, shear)):
+        late.append(
+            pltpu.make_async_copy(source, target, small_sem.at[len(small) + len(late)])
+        )
+        late[-1].start()
 
     sibling = (brick, 1 - shard)
     partners = []
@@ -109,6 +134,8 @@
     own_node = lanes // nodes == sublanes
     width = 2 * nodes
 
+    for copy in small:
+        copy.wait()
     block_row = blocks[...].astype(jnp.float32)
     block_column = column_of(block_row)
     face_rows = faces[...].astype(jnp.float32)
@@ -187,6 +214,8 @@
     for copy in copies:
         copy.start()
     total = select_sum(same_here, pieces)
+    for copy in late:
+        copy.wait()
     copies[0].wait()
     copies[1].wait()
     same_there = equal(block_column, other_blocks[...].astype(jnp.float32))
@@ -207,18 +236,25 @@
     floor = jnp.maximum(node_mass, FLOOR)
     bound = jnp.where(brick == 0, float(NB // 8), 0.0)
     fixed = block_column < bound
-    speeds = [jnp.where(fixed, 0.0, q / floor) for q in moment]
-
-    for g in range(groups):
+    for c in range(3):
+        speeds_out[c] = jnp.where(fixed, 0.0, moment[c] / floor)
+
+
+def return_kernel(
+    speeds, weights, grads, stress, lame, shear, moved_out, stress_out, moved, updated, sems
+):
+    tiles, nodes, parts = weights.shape
+    lanes = lax.broadcasted_iota(jnp.int32, (GROUP, GROUP * nodes), 1)
+    sublanes = lax.broadcasted_iota(jnp.int32, (GROUP, GROUP * nodes), 0)
+    own_node = lanes // nodes == sublanes
+    pending = []
+    span = tiles // SPANS
+    for g in range(tiles // GROUP):
         rows = pl.ds(g * GROUP, GROUP)
         left = jnp.concatenate(
             [
-                jnp.where(
-                    own_node,
-                    jnp.concatenate([s[g * GROUP : (g + 1) * GROUP]] * (GROUP // 2), 1),
-                    0.0,
-                )
-                for s in speeds
+                jnp.where(own_node, jnp.concatenate([speeds[c, rows]] * (GROUP // 2), 1), 0.0)
+                for c in range(3)
             ],
             0,
         ).astype(jnp.bfloat16)
@@ -233,16 +269,27 @@
             return out[i * GROUP : (i + 1) * GROUP, q * parts : (q + 1) * parts]
 
         for c in range(3):
-            moved_out[c, rows] = block(c, 0)
+            moved[c, rows] = block(c, 0)
         trace = block(0, 1) + block(1, 2) + block(2, 3)
         bulk = STEP * (lame[rows] * trace)
         twist = (2.0 * STEP) * shear[rows]
         for s, (i, j) in enumerate(SIX):
             if i == j:
-                stress_out[s, rows] = stress[s, rows] + (bulk + twist * block(i, j + 1))
+                updated[s, rows] = stress[s, rows] + (bulk + twist * block(i, j + 1))
             else:
                 rate = 0.5 * (block(i, j + 1) + block(j, i + 1))
-                stress_out[s, rows] = stress[s, rows] + twist * rate
+                updated[s, rows] = stress[s, rows] + twist * rate
+        if (g + 1) * GROUP % span == 0:
+            part = pl.ds((g + 1) * GROUP - span, span)
+            n = len(pending)
+            for q, (source, target) in enumerate(((moved, moved_out), (updated, stress_out))):
+                copy = pltpu.make_async_copy(
+                    source.at[:, part], target.at[:, part], sems.at[n // 2, q]
+                )
+                copy.start()
+                pending.append(copy)
+    for copy in pending:
+        copy.wait()
 
 
 def on_device(
@@ -263,34 +310,11 @@
     faces = cuts * face_count
     groups = tiles // GROUP
     vmem = pl.BlockSpec(memory_space=pltpu.VMEM)
-    hbm = pl.BlockSpec(memory_space=pl.ANY)
-    f32 = jnp.float32
+    hbm = pl.BlockSpec(memory_space=pltpu.HBM)
+    f32, bf16 = jnp.float32, jnp.bfloat16
     dma = pltpu.SemaphoreType.DMA
-    moved, updated = pl.pallas_call(
-        kernel,
-        out_shape=(
-            jax.ShapeDtypeStruct((3, tiles, parts), f32),
-            jax.ShapeDtypeStruct((6, tiles, parts), f32),
-        ),
-        in_specs=[vmem] * 6 + [hbm] * 2 + [vmem] * 2,
-        out_specs=(vmem, vmem),
-        scratch_shapes=[
-            pltpu.VMEM((tiles, nodes, parts), jnp.bfloat16),
-            pltpu.VMEM((3, tiles, nodes, parts), jnp.bfloat16),
-            pltpu.VMEM((tiles, 4 * nodes), f32),
-            pltpu.VMEM((faces, 4 * nodes), f32),
-            pltpu.VMEM((tiles, 4 * nodes), f32),
-            pltpu.VMEM((1, tiles), jnp.int32),
-            pltpu.VMEM((2, faces, 4 * nodes), f32),
-            dma((groups, 2)),
-            dma((2,)),
-            dma((2,)),
-            dma((2, cuts)),
-            dma((2, cuts)),
-        ],
-        compiler_params=pltpu.CompilerParams(collective_id=0, has_side_effects=True),
-        name="step",
-    )(
+    shaped = jax.ShapeDtypeStruct
+    inputs = (
         velocity.reshape(3, tiles, parts),
         particle_mass.reshape(tiles, parts),
         particle_volume.reshape(tiles, parts),
@@ -302,6 +326,56 @@
         tile_block,
         face_blocks[0],
     )
+    held = pl.pallas_call(
+        exchange_kernel,
+        out_shape=(
+            shaped((3, tiles, 2 * nodes), f32),
+            shaped((tiles, nodes, parts), bf16),
+            shaped((3, tiles, nodes, parts), bf16),
+            shaped((6, tiles, parts), f32),
+            shaped((tiles, parts), f32),
+            shaped((tiles, parts), f32),
+        ),
+        in_specs=[hbm] * 10,
+        out_specs=[vmem] * 6,
+        scratch_shapes=[
+            pltpu.VMEM((3, tiles, parts), f32),
+            pltpu.VMEM((tiles, parts), f32),
+            pltpu.VMEM((tiles, parts), f32),
+            pltpu.VMEM((1, tiles), jnp.int32),
+            pltpu.VMEM((cuts, face_count), jnp.int32),
+            pltpu.VMEM((tiles, 4 * nodes), f32),
+            pltpu.VMEM((faces, 4 * nodes), f32),
+            pltpu.VMEM((tiles, 4 * nodes), f32),
+            pltpu.VMEM((1, tiles), jnp.int32),
+            pltpu.VMEM((2, faces, 4 * nodes), f32),
+            dma((8,)),
+            dma((groups, 2)),
+            dma((2,)),
+            dma((2,)),
+            dma((2, cuts)),
+            dma((2, cuts)),
+        ],
+        compiler_params=pltpu.CompilerParams(
+            collective_id=0, has_side_effects=True, vmem_limit_bytes=VMEM_LIMIT
+        ),
+        name="exchange",
+    )(
+        *(pltpu.with_memory_space_constraint(x, pltpu.HBM) for x in inputs)
+    )
+    moved, updated = pl.pallas_call(
+        return_kernel,
+        out_shape=(shaped((3, tiles, parts), f32), shaped((6, tiles, parts), f32)),
+        in_specs=[vmem] * 6,
+        out_specs=[hbm] * 2,
+        scratch_shapes=[
+            pltpu.VMEM((3, tiles, parts), f32),
+            pltpu.VMEM((6, tiles, parts), f32),
+            dma((SPANS, 2)),
+        ],
+        compiler_params=pltpu.CompilerParams(vmem_limit_bytes=VMEM_LIMIT),
+        name="bring_back",
+    )(*held)
     return moved.reshape(3, 1, -1), updated.reshape(6, 1, -1)
 
 

time: 16.9 us -> 13.7 us (0.81)
  local copies, waits for them, and re-layouts: 3.16 us -> 0 us
    unnamed x2 -> x0, local copies, waits for them, and re-layouts: 3.16 us -> none
    pallas_call x1 -> x2, Pallas kernels: 12.9 us -> 12.9 us  [the longest x1 11.5 us: on_device(): pl.pallas_call(exchange_kernel, out_shape=(shaped((3, tiles, 2 * nodes),...]
where the time goes in v2:
time: 13.7 us; the launch traced here: 13.5 us
  Pallas kernels  12.9 us (94%)
  between operations  0.64 us (5%)
    pallas_call x1, Pallas kernels, on_device(): pl.pallas_call(exchange_kernel, out_shape=(shaped((3, tiles, 2 * nodes),...  11.5 us
    pallas_call x1, Pallas kernels, on_device(): pl.pallas_call(return_kernel, out_shape=(shaped((3, tiles, parts), f32),...  1.41 us

profile of v2, /device:TPU:0, one launch (start us, length us, event | category | flops | bytes accessed | tf_op | source)
XLA Modules:
  0.0 13.5 jit_solution(5100562354454900593)
XLA Ops:
  0.6 11.5 %exchange.1 = (f32[3,64,128]{2,1,0:T(8,128)S(1)}, bf16[64,64,128]{2,1,0:T(8,128)(2,1)S(1)}, bf16[3,64,64,128]{3,2,1,0:T(8,128)(2,1)S(1)}, f32[6,64,128]{2,1,0:T(...) custom-call(f32[3,64,128]{2,1,0:T(8,128)} %bitcast.14, f32[64,128]{1,0:T(8,128)} %bitcast.15, ...), custom_call_target="tpu_custom_call" | custom-call | tf_op jit(solution)/shard_map/exchange/pallas_call | solution.py:329
  12.1 1.4 %bring_back.1 = (f32[3,64,128]{2,1,0:T(8,128)}, f32[6,64,128]{2,1,0:T(8,128)}) custom-call(f32[3,64,128]{2,1,0:T(8,128)S(1)} %get-tuple-element.10.speeds, bf16[64,64,128]{2,1,0:T(8,128)(2,1)S(1)} %get-tuple-element.11.weights, bf16[3,64,64,128]{3,2,1,0:T(8,128)(2,1)S(1)} %get-tuple-element.12.grads, f32[6,64,128]{2,1,0:T(8,128)S(1)} %get-tuple-element.13.stress, ...), custom_call_target="tpu_custom_call" | custom-call | tf_op jit(solution)/shard_map/bring_back/pallas_call | solution.py:366

commit v3 on v2

--- a/solution.py
+++ b/solution.py
@@ -11,6 +11,7 @@
 MESH = pl.DeviceIdType.MESH
 GROUP = 8
 SPANS = 4
+STREAMED = 2
 VMEM_LIMIT = 16 * 2**20
 PAIRING = ((0, 3, 5), (3, 1, 4), (5, 4, 2))
 SIX = ((0, 0), (1, 1), (2, 2), (0, 1), (1, 2), (0, 2))
@@ -48,6 +49,13 @@
 
 def equal(column, row):
     return jnp.where(column == row, 1.0, 0.0).astype(jnp.bfloat16)
+
+
+def side_by_side(weights, grads, rows):
+    size = weights[rows].shape
+    flat = (size[0] * size[1], size[2])
+    parts = [weights[rows].reshape(flat)] + [grads[j, rows].reshape(flat) for j in range(3)]
+    return jnp.concatenate(parts, 1)
 
 
 def exchange_kernel(
@@ -129,9 +137,10 @@
     for device in greeted:
         pl.semaphore_signal(barrier, inc=1, device_id=device, device_id_type=MESH)
 
-    lanes = lax.broadcasted_iota(jnp.int32, (GROUP, GROUP * nodes), 1)
-    sublanes = lax.broadcasted_iota(jnp.int32, (GROUP, GROUP * nodes), 0)
-    own_node = lanes // nodes == sublanes
+    own_node = (
+        lax.broadcasted_iota(jnp.int32, (GROUP, GROUP * nodes), 1) // nodes
+        == lax.broadcasted_iota(jnp.int32, (GROUP, GROUP * nodes), 0)
+    )
     width = 2 * nodes
 
     for copy in small:
@@ -145,36 +154,62 @@
     tile_of_face = equal(face_column, block_row)
     same_here = equal(block_column, block_row)
 
+    packed = parts // (4 * GROUP)
+    lane = lax.broadcasted_iota(jnp.int32, (nodes, parts), 1)
+    lane_tile = lane // (4 * GROUP) * GROUP + lane % GROUP
     first_half = lax.broadcasted_iota(jnp.int32, (GROUP, width), 1) < nodes
-    for g in range(groups):
-        rows = pl.ds(g * GROUP, GROUP)
-        for copy in loads[g]:
-            copy.wait()
-        m = mass[rows]
-        zero = jnp.zeros_like(m)
-        columns = [jnp.concatenate([m] + [m * velocity[c, rows] for c in range(3)], 0)]
-        vol = volume[rows]
-        scaled = [(-STEP) * (vol * stress[s, rows]) for s in range(6)]
-        for j in range(3):
-            columns.append(jnp.concatenate([zero] + [scaled[PAIRING[i][j]] for i in range(3)], 0))
-        left = jnp.concatenate([column.astype(jnp.bfloat16) for column in columns], 1)
-        right = jnp.concatenate(
-            [weights[rows].reshape(GROUP * nodes, parts)]
-            + [grads[j, rows].reshape(GROUP * nodes, parts) for j in range(3)],
-            1,
+    for h in range(groups // packed):
+        stacked = []
+        for g in range(h * packed, (h + 1) * packed):
+            rows = pl.ds(g * GROUP, GROUP)
+            m = mass[rows]
+            zero = jnp.zeros_like(m)
+            vol = volume[rows]
+            scaled = [(-STEP) * (vol * stress[s, rows]) for s in range(6)]
+            columns = [jnp.concatenate([m] + [m * velocity[c, rows] for c in range(3)], 0)]
+            for j in range(3):
+                columns.append(
+                    jnp.concatenate([zero] + [scaled[PAIRING[i][j]] for i in range(3)], 0)
+                )
+            stacked.append(jnp.concatenate(columns, 1))
+        right = jnp.concatenate(stacked, 0).astype(jnp.bfloat16)
+        kept = jnp.zeros((nodes, parts), jnp.float32)
+        first = h * packed
+        for g in range(first, first + packed):
+            for copy in loads[g]:
+                copy.wait()
+        rows = pl.ds(first * GROUP, STREAMED * GROUP)
+        sums = lax.dot_general(
+            side_by_side(weights, grads, rows),
+            right,
+            (((1,), (1,)), ((), ())),
+            preferred_element_type=jnp.float32,
         )
-        out = lax.dot_general(
-            left, right, (((1,), (1,)), ((), ())), preferred_element_type=jnp.float32
-        )
-        twice = []
-        for c in range(4):
-            piece = jnp.where(own_node, out[c * GROUP : (c + 1) * GROUP], 0.0)
-            total = piece[:, :width]
-            for q in range(1, GROUP // 2):
-                total = total + piece[:, q * width : (q + 1) * width]
-            twice.append(total + pltpu.roll(total, nodes, 1))
-        own_sums[rows, :width] = jnp.where(first_half, twice[0], twice[1])
-        own_sums[rows, width:] = jnp.where(first_half, twice[2], twice[3])
+        for g in range(first + STREAMED, first + packed):
+            rows = pl.ds(g * GROUP, GROUP)
+            out = lax.dot_general(
+                right[(g - first) * 4 * GROUP : (g - first + 1) * 4 * GROUP],
+                side_by_side(weights, grads, rows),
+                (((1,), (1,)), ((), ())),
+                preferred_element_type=jnp.float32,
+            )
+            twice = []
+            for c in range(4):
+                piece = jnp.where(own_node, out[c * GROUP : (c + 1) * GROUP], 0.0)
+                total = piece[:, :width]
+                for q in range(1, GROUP // 2):
+                    total = total + piece[:, q * width : (q + 1) * width]
+                twice.append(total + pltpu.roll(total, nodes, 1))
+            own_sums[rows, :width] = jnp.where(first_half, twice[0], twice[1])
+            own_sums[rows, width:] = jnp.where(first_half, twice[2], twice[3])
+        for t in range(STREAMED * GROUP):
+            kept = jnp.where(lane_tile == t, sums[t * nodes : (t + 1) * nodes], kept)
+        turned = jnp.transpose(jnp.concatenate([kept, kept], 0))
+        for g in range(STREAMED):
+            rows = pl.ds((h * packed + g) * GROUP, GROUP)
+            twice = [turned[(4 * g + c) * GROUP : (4 * g + c + 1) * GROUP] for c in range(4)]
+            own_sums[rows, :width] = jnp.where(first_half, twice[0], twice[1])
+            own_sums[rows, width:] = jnp.where(first_half, twice[2], twice[3])
 
     pieces = own_sums[...]
     face_sums[...] = select_sum(tile_of_face, pieces)
@@ -233,11 +268,11 @@
         jnp.where(half, two, two_turned),
         jnp.where(half, two_turned, two) - STEP * node_mass,
     ]
-    floor = jnp.maximum(node_mass, FLOOR)
+    inverse = 1.0 / jnp.maximum(node_mass, FLOOR)
     bound = jnp.where(brick == 0, float(NB // 8), 0.0)
     fixed = block_column < bound
     for c in range(3):
-        speeds_out[c] = jnp.where(fixed, 0.0, moment[c] / floor)
+        speeds_out[c] = jnp.where(fixed, 0.0, moment[c] * inverse)
 
 
 def return_kernel(

time: 13.7 us -> 12.5 us (0.912)
  Pallas kernels: 12.9 us -> 11.7 us
    pallas_call x1, Pallas kernels: 11.5 us -> 10.3 us  [on_device(): pl.pallas_call(exchange_kernel, out_shape=(shaped((3, tiles, 2 * nodes),...]
where the time goes in v3:
time: 12.5 us; the launch traced here: 12.4 us
  Pallas kernels  11.7 us (94%)
  between operations  0.64 us (5%)
    pallas_call x1, Pallas kernels, on_device(): pl.pallas_call(exchange_kernel, out_shape=(shaped((3, tiles, 2 * nodes),...  10.3 us
    pallas_call x1, Pallas kernels, on_device(): pl.pallas_call(return_kernel, out_shape=(shaped((3, tiles, parts), f32),...  1.41 us

profile of v3, /device:TPU:0, one launch (start us, length us, event | category | flops | bytes accessed | tf_op | source)
XLA Modules:
  0.0 12.4 jit_solution(13151014879747855190)
XLA Ops:
  0.6 10.3 %exchange.1 = (f32[3,64,128]{2,1,0:T(8,128)S(1)}, bf16[64,64,128]{2,1,0:T(8,128)(2,1)S(1)}, bf16[3,64,64,128]{3,2,1,0:T(8,128)(2,1)S(1)}, f32[6,64,128]{2,1,0:T(...) custom-call(f32[3,64,128]{2,1,0:T(8,128)} %bitcast.14, f32[64,128]{1,0:T(8,128)} %bitcast.15, ...), custom_call_target="tpu_custom_call" | custom-call | tf_op jit(solution)/shard_map/exchange/pallas_call | solution.py:364
  10.9 1.4 %bring_back.1 = (f32[3,64,128]{2,1,0:T(8,128)}, f32[6,64,128]{2,1,0:T(8,128)}) custom-call(f32[3,64,128]{2,1,0:T(8,128)S(1)} %get-tuple-element.10.speeds, bf16[64,64,128]{2,1,0:T(8,128)(2,1)S(1)} %get-tuple-element.11.weights, bf16[3,64,64,128]{3,2,1,0:T(8,128)(2,1)S(1)} %get-tuple-element.12.grads, f32[6,64,128]{2,1,0:T(8,128)S(1)} %get-tuple-element.13.stress, ...), custom_call_target="tpu_custom_call" | custom-call | tf_op jit(solution)/shard_map/bring_back/pallas_call | solution.py:401
